TPU v7x, 32 devices: a whole 2x2x4 slice. The times are simulated.
32 devices in a mesh: groups: 2 (over x), chan: 16 (over z, y, core).
Axes of the slice: x: 2, y: 2, z: 4, core: 2. Of those that a mesh axis runs over, the one named last changes fastest.
Arguments:
- data: bfloat16 [28672, 4096], P(('groups', 'chan')), parts along dimension 0, as said below
- alive: int32 [8192], P(('groups', 'chan')), parts along dimension 0, may hold values 0 or 1
- sources: int32 [2, 16], replicated, may hold values from 0 to 4095, as said below
Outputs:
- correlations: bfloat16 [4, 16, 256, 4096], P('groups', None, None, 'chan'), parts along dimension 0
There are 2 independent parts, one for each index of `groups`. A program takes and returns all parts, laid end to end along the dimension named above; an argument that names none is the same for every part. Nothing has to cross between parts.
Inputs may be any that keep to these rules, and one draw needn't show every extreme that they name: `sources`: no channel number appears twice in the array, and channel 4096 - 1 is always one of them. `data`: samples have channel and time-block scales of their own.
All inputs are finite; a program needn't handle non-finite values. No bound on the sum of `alive` on one device may be relied on, other than what follows from the above.
Results may differ from a plain program's by a relative error of at most 0.0076.
Values may be sent and summed in bfloat16 or wider, within the bound.
No kernel may reach another device: no remote copies, remote signals or barrier semaphores. Data moves between devices by JAX's collectives and lax.ppermute only.
A program may use at most 128 MiB of HBM per device.

v0:
```python
import math
import jax
import jax.numpy as jnp
from jax import lax
from jax.sharding import PartitionSpec as P

SEGMENT_LENGTH = 512
NF = 128
LAGS = 256
SRC = 16
ROUNDS = 2
SEGMENT_TALLY = 28


def forward_table():
    times = jnp.arange(SEGMENT_LENGTH, dtype=jnp.int32)[:, None]
    bins = jnp.arange(NF, dtype=jnp.int32)[None, :] + 1
    angle = 2.0 * math.pi / SEGMENT_LENGTH * (bins * times % SEGMENT_LENGTH).astype(jnp.float32)
    table = jnp.concatenate([jnp.cos(angle), -jnp.sin(angle)], axis=1) / math.sqrt(SEGMENT_LENGTH)
    return table.astype(jnp.bfloat16)


def inverse_table():
    shifts = jnp.arange(LAGS, dtype=jnp.int32)[:, None] - LAGS // 2
    bins = jnp.arange(NF, dtype=jnp.int32)[None, :] + 1
    angle = 2.0 * math.pi / SEGMENT_LENGTH * (bins * shifts % SEGMENT_LENGTH).astype(jnp.float32)
    return jnp.concatenate([jnp.cos(angle), -jnp.sin(angle)], axis=1).astype(jnp.bfloat16)


def body(data, alive, sources):
    count = lax.axis_size("chan")
    width = data.shape[1] // count
    table = forward_table()
    split = data.reshape(data.shape[0], count, width)
    moved = lax.all_to_all(split, "chan", split_axis=1, concat_axis=0, tiled=True)
    blocks = moved.reshape(SEGMENT_TALLY, SEGMENT_LENGTH, moved.shape[2])
    spectra = jnp.einsum("tk,wtc->wkc", table, blocks, preferred_element_type=jnp.float32)
    level = jnp.mean(spectra[:, :NF] ** 2 + spectra[:, NF:] ** 2, axis=0)
    factor = alive.astype(jnp.float32)[None, :] / jnp.sqrt(level + 0.01)
    factor = jnp.concatenate([factor, factor], axis=0)
    whitened = (spectra * factor[None]).astype(jnp.bfloat16)
    ids = sources.reshape(-1)
    owner = ids // width
    local = ids % width
    mine = owner == lax.axis_index("chan")
    picked = jnp.transpose(jnp.take(whitened, local, axis=2), (2, 0, 1)).astype(jnp.float32)
    picked = jnp.where(mine[:, None, None], picked, 0.0)
    src = lax.psum(picked, "chan").astype(jnp.bfloat16)
    src_re, src_im = (src[:, :, :NF], src[:, :, NF:])
    own_re, own_im = (whitened[:, :NF], whitened[:, NF:])
    form = "qwf,wfc->qfc"
    correlogram_realpart = jnp.einsum(
        form, src_re, own_re, preferred_element_type=jnp.float32
    ) + jnp.einsum(form, src_im, own_im, preferred_element_type=jnp.float32)
    cross_imaginary = jnp.einsum(
        form, src_re, own_im, preferred_element_type=jnp.float32
    ) - jnp.einsum(form, src_im, own_re, preferred_element_type=jnp.float32)
    cross = jnp.concatenate([correlogram_realpart, cross_imaginary], axis=1).astype(jnp.bfloat16)
    lagged = jnp.einsum("lk,qkc->qlc", inverse_table(), cross, preferred_element_type=jnp.float32)
    lagged = lagged / math.sqrt(NF * SEGMENT_TALLY)
    return lagged.reshape(ROUNDS, SRC, LAGS, width).astype(jnp.bfloat16)


def solution(mesh):
    return jax.shard_map(
        body,
        mesh=mesh,
        in_specs=(P(("groups", "chan"), None), P(("groups", "chan")), P()),
        out_specs=P("groups", None, None, "chan"),
        check_vma=False,
    )
```

profile of v0, /device:TPU:0, one launch (start us, length us, event | category | flops | bytes accessed | tf_op | source)
XLA Modules:
  0.0 326.9 jit_solution(7985542122648060904)
XLA Ops:
  0.0 6.9 %copy.27 = bf16[112,16,8,256]{3,2,0,1:T(8,128)(2,1)} copy(bf16[112,16,8,256]{3,2,1,0:T(8,128)(2,1)} %bitcast.32) | data formatting | bytes 14680064 | tf_op jit(solution)/shard_map/reshape | solution.py:34
  6.9 0.0 copy-start.3
  6.9 0.0 copy-start.2
  6.9 7.6 %all-to-all-start = ((bf16[896,16,256]{2,0,1:T(8,128)(2,1)}), bf16[896,16,256]{2,0,1:T(8,128)(2,1)}, u32[]{:S(2)}, u32[]{:S(2)}) async-start(bf16[896,16,256]{2,0,1:T(8,128)(2,1)} %bitcast.31), calls=%async_computation | async-start | bytes 14680064 | tf_op jit(solution)/shard_map/all_to_all | solution.py:35
  14.4 0.0 copy-done.3
  14.4 0.1 reshape.125
  14.5 0.1 reshape.124
  14.6 0.0 copy-done.2
  14.7 0.6 cosine_convert_fusion
  15.3 1.1 fusion.33
  16.4 130.5 %all-to-all-done = bf16[896,16,256]{2,0,1:T(8,128)(2,1)} async-done(((bf16[896,16,256]{2,0,1:T(8,128)(2,1)}), bf16[896,16,256]{2,0,1:T(8,128)(2,1)}, u32[]{:S(2)}, u32[]{:S(2)}) %all-to-all-start) | async-done | bytes 7340064 | tf_op jit(solution)/shard_map/all_to_all | solution.py:35
  146.9 5.2 %convolution_bitcast_fusion = f32[28,256,256]{2,1,0:T(8,128)S(1)} fusion(bf16[28,512,256]{2,1,0:T(8,128)(2,1)} %bitcast.3, f32[512,128]{0,1:T(8,128)S(1)} %get-tuple-element.14, f32[512,128]{0,1:T(8,128)S(1)} %get-tuple-element.13), kind=kOutput, calls=%fused_computation.14 | convolution fusion | flops 1879441408 | bytes 15204352 | tf_op jit(solution)/shard_map/tk,wtc->wkc/dot_general | solution.py:37
  152.0 0.5 fusion.5
  152.6 2.6 multiply_convert_fusion.1
  155.2 7.7 %copy.7 = bf16[28,256,256]{1,0,2:T(8,128)(2,1)} copy(bf16[28,256,256]{2,1,0:T(8,128)(2,1)} %multiply_convert_fusion.1) | data formatting | bytes 7340032 | tf_op jit(solution)/shard_map/convert_element_type | solution.py:41
  162.9 3.6 %fusion.40 = (bf16[28,128,256]{2,1,0:T(8,128)(2,1)S(1)}, bf16[28,128,256]{2,1,0:T(8,128)(2,1)}) fusion(bf16[28,256,256]{2,1,0:T(8,128)(2,1)} %multiply_convert_fusion.1), kind=kLoop, calls=%fused_computation.76 | loop fusion | bytes 7340032 | tf_op jit(solution)/shard_map/slice | solution.py:50
  166.6 2.8 gather_fusion
  169.3 0.2 convert_select_fusion
  169.6 100.6 %all-reduce.1 = bf16[32,28,256]{2,1,0:T(8,128)(2,1)S(1)} all-reduce(f32[32,28,256]{2,1,0:T(8,128)S(1)} %convert_select_fusion), channel_id=1, replica_groups=mesh['groups'=2,'chan'=16] {'chan'}, use_global_device_ids=true, to_apply=%region_1.2 | all-reduce | flops 229376 | bytes 1376256 | tf_op jit(solution)/shard_map/psum | solution.py:48
  270.2 0.1 fusion.41
  270.3 2.6 copy.13
  272.8 1.6 copy.10
  274.5 0.0 copy-start
  274.5 0.0 copy-start.1
  274.5 4.6 %fusion.14 = f32[128,256,32]{1,2,0:T(8,128)} fusion(bf16[32,28,128]{0,1,2:T(8,128)(2,1)} %copy.13, bf16[28,128,256]{2,1,0:T(8,128)(2,1)S(1)} %get-tuple-element.5), kind=kOutput, calls=%fused_computation.21 | convolution fusion | flops 58720256 | bytes 6258688 | tf_op jit(solution)/shard_map/qwf,wfc->qfc/dot_general | solution.py:57
  279.1 0.0 copy-done
  279.1 0.0 copy-done.1
  279.1 3.2 fusion.12
  282.4 3.3 fusion.10
  285.6 3.3 %fusion.16 = f32[128,256,32]{1,2,0:T(8,128)} fusion(bf16[32,28,128]{0,1,2:T(8,128)(2,1)S(1)} %copy.10, bf16[28,128,256]{2,1,0:T(8,128)(2,1)S(1)} %get-tuple-element.5), kind=kOutput, calls=%fused_computation.23 | convolution fusion | flops 58720256 | bytes 6258688 | tf_op jit(solution)/shard_map/qwf,wfc->qfc/dot_general | solution.py:52
  288.9 5.3 %copy.16 = f32[128,256,32]{0,1,2:T(8,128)} copy(f32[128,256,32]{1,2,0:T(8,128)} %fusion.14) | data formatting | bytes 8388608 | tf_op jit(solution)/shard_map/qwf,wfc->qfc/dot_general | solution.py:57
  294.2 5.3 %copy.15 = f32[128,256,32]{0,1,2:T(8,128)} copy(f32[128,256,32]{1,2,0:T(8,128)} %fusion.10) | data formatting | bytes 8388608 | tf_op jit(solution)/shard_map/qwf,wfc->qfc/dot_general | solution.py:55
  299.6 5.3 %copy.14 = f32[128,256,32]{0,1,2:T(8,128)} copy(f32[128,256,32]{1,2,0:T(8,128)} %fusion.12) | data formatting | bytes 8388608 | tf_op jit(solution)/shard_map/qwf,wfc->qfc/dot_general | solution.py:54
  304.9 5.3 %copy.11 = f32[128,256,32]{0,1,2:T(8,128)} copy(f32[128,256,32]{1,2,0:T(8,128)} %fusion.16) | data formatting | bytes 8388608 | tf_op jit(solution)/shard_map/qwf,wfc->qfc/dot_general | solution.py:52
  310.2 7.6 %fusion.8 = (bf16[32,128,256]{1,2,0:T(8,128)(2,1)S(1)}, bf16[32,128,256]{1,2,0:T(8,128)(2,1)S(1)}) fusion(f32[128,256,32]{0,1,2:T(8,128)} %copy.11, f32[128,256,32]{0,1,2:T(8,128)} %copy.14, f32[128,256,32]{0,1,2:T(8,128)} %copy.15, f32[128,256,32]{0,1,2:T(8,128)} %copy.16), kind=kLoop, calls=%fused_computation.15 | loop fusion | flops 4194304 | bytes 20971520 | tf_op jit(solution)/shard_map/add | solution.py:52
  317.8 2.9 multiply_convert_fusion
  320.7 6.2 %copy.8 = bf16[2,16,256,256]{3,2,1,0:T(8,128)(2,1)} copy(bf16[2,16,256,256]{2,3,1,0:T(8,128)(2,1)} %bitcast.33) | data formatting | bytes 8388608 | tf_op jit(solution)/shard_map/convert_element_type | solution.py:61
  (8 shorter events, 0.1 us)
Async XLA Ops:
  6.9 7.6 %copy-start.3 = (s32[2,16]{1,0:T(2,128)S(1)}, s32[2,16]{1,0:T(2,128)}, u32[]{:S(2)}) copy-start(s32[2,16]{1,0:T(2,128)} %param.5) | copy-start | bytes 388
  6.9 7.8 %copy-start.2 = (s32[256]{0:T(256)S(1)}, s32[256]{0:T(256)}, u32[]{:S(2)}) copy-start(s32[256]{0:T(256)} %param.4) | copy-start | bytes 3076
  6.9 140.0 %all-to-all-start = ((bf16[896,16,256]{2,0,1:T(8,128)(2,1)}), bf16[896,16,256]{2,0,1:T(8,128)(2,1)}, u32[]{:S(2)}, u32[]{:S(2)}) async-start(bf16[896,16,256]{2,0,1:T(8,128)(2,1)} %bitcast.31), calls=%async_computation | async-start | bytes 14680064 | tf_op jit(solution)/shard_map/all_to_all | solution.py:35
  274.5 4.7 %copy-start = (bf16[28,128,256]{2,1,0:T(8,128)(2,1)S(1)}, bf16[28,128,256]{2,1,0:T(8,128)(2,1)}, u32[]{:S(2)}) copy-start(bf16[28,128,256]{2,1,0:T(8,128)(2,1)} %get-tuple-element.6) | copy-start | bytes 5505028
  274.5 4.7 %copy-start.1 = (bf16[32,28,128]{0,1,2:T(8,128)(2,1)S(1)}, bf16[32,28,128]{0,1,2:T(8,128)(2,1)}, u32[]{:S(2)}) copy-start(bf16[32,28,128]{0,1,2:T(8,128)(2,1)} %copy.13) | copy-start | bytes 688132
where the time goes:
time: 328 us; the launch traced here: 327 us
  waiting for transfers between devices  130 us (40%)
  blocking collectives  101 us (31%)
  local copies, waits for them, and re-layouts  52.9 us (16%)
  matrix products  22.5 us (7%)
  other arithmetic  12.8 us (4%)
  starting transfers between devices  7.56 us (2%)
    all_to_all x1, waiting for transfers between devices, body(): lax.all_to_all(split, 'chan', split_axis=1, concat_axis=0, tiled=True)  130 us
    psum x1, blocking collectives, body(): src = lax.psum(picked, 'chan').astype(jnp.bfloat16)  101 us
    convert_element_type x1, local copies, waits for them, and re-layouts, body(): whitened = (spectra * factor[None]).astype(jnp.bfloat16)  7.7 us
    add x1, other arithmetic, body(): jnp.einsum(form, src_re, own_re, preferred_element_type=jnp.float32)  7.63 us
    all_to_all x1, starting transfers between devices, body(): lax.all_to_all(split, 'chan', split_axis=1, concat_axis=0, tiled=True)  7.56 us
    reshape x1, local copies, waits for them, and re-layouts, body(): split = data.reshape(data.shape[0], count, width)  6.85 us
  transfers between devices with their start and end apart: 1, of which 1 were waited for; matrix products, arithmetic and copies ran while one was open for 1% of the time, Pallas kernels for 0%

commit v1 on v0

--- a/solution.py
+++ b/solution.py
@@ -3,6 +3,7 @@
 import jax.numpy as jnp
 from jax import lax
 from jax.sharding import PartitionSpec as P
+from jax.lax import all_to_all, axis_size
 
 SEGMENT_LENGTH = 512
 NF = 128
@@ -10,6 +11,14 @@
 SRC = 16
 ROUNDS = 2
 SEGMENT_TALLY = 28
+
+
+def play_sample(mesh_name, block_in):
+    now = axis_size(mesh_name)
+    tall = jnp.split(block_in, now, axis=1)
+    small = jnp.stack(tall)
+    view_out = all_to_all(small, axis_name=mesh_name, split_axis=0, concat_axis=0)
+    return jnp.concatenate(view_out, axis=0)
 
 
 def forward_table():
@@ -32,7 +41,7 @@
     width = data.shape[1] // count
     table = forward_table()
     split = data.reshape(data.shape[0], count, width)
-    moved = lax.all_to_all(split, "chan", split_axis=1, concat_axis=0, tiled=True)
+    moved = play_sample("chan", split)
     blocks = moved.reshape(SEGMENT_TALLY, SEGMENT_LENGTH, moved.shape[2])
     spectra = jnp.einsum("tk,wtc->wkc", table, blocks, preferred_element_type=jnp.float32)
     level = jnp.mean(spectra[:, :NF] ** 2 + spectra[:, NF:] ** 2, axis=0)

time: 328 us -> 360 us (1.098)
  blocking collectives: 101 us -> 123 us
  local copies, waits for them, and re-layouts: 52.9 us -> 72.6 us
  other arithmetic: 12.8 us -> 6.3 us
  matrix products: 22.5 us -> 16.9 us
    unnamed x8 -> x26, local copies, waits for them, and re-layouts: 0.02 us -> 32.1 us
    psum x1, blocking collectives: 101 us -> 123 us  [body(): src = lax.psum(picked, 'chan').astype(jnp.bfloat16)]
    dot_general x4 -> x0, local copies, waits for them, and re-layouts: 21.3 us -> none  [the longest x1 5.34 us: body(): jnp.einsum(form, src_re, own_im, preferred_element_type=jnp.float32)]
    all_to_all x0 -> x1, local copies, waits for them, and re-layouts: none -> 11.2 us  [play_sample(): all_to_all(small, axis_name=mesh_name, split_axis=0, concat_axis=0)]
    slice x1 -> x3, local copies, waits for them, and re-layouts: 3.64 us -> 11.8 us  [body(): own_re, own_im = (whitened[:, :NF], whitened[:, NF:])]
    add x1 -> x0, other arithmetic: 7.63 us -> none  [body(): jnp.einsum(form, src_re, own_re, preferred_element_type=jnp.float32)]
    reshape x1 -> x0, local copies, waits for them, and re-layouts: 6.85 us -> none  [body(): split = data.reshape(data.shape[0], count, width)]
    dot_general x1, matrix products: 2.88 us -> 7.23 us  [body(): jnp.einsum('lk,qkc->qlc', inverse_table(), cross, preferred_element_type=...]
where the time goes in v1:
time: 360 us; the launch traced here: 357 us
  waiting for transfers between devices  131 us (36%)
  blocking collectives  123 us (34%)
  local copies, waits for them, and re-layouts  72.6 us (20%)
  matrix products  16.9 us (5%)
  starting transfers between devices  7.56 us (2%)
  other arithmetic  6.3 us (2%)
    all_to_all x1, waiting for transfers between devices, play_sample(): all_to_all(small, axis_name=mesh_name, split_axis=0, concat_axis=0)  131 us
    psum x1, blocking collectives, body(): src = lax.psum(picked, 'chan').astype(jnp.bfloat16)  123 us
    unnamed x26, local copies, waits for them, and re-layouts  32.1 us
    slice x3, local copies, waits for them, and re-layouts, body(): own_re, own_im = (whitened[:, :NF], whitened[:, NF:])  11.8 us
    all_to_all x1, local copies, waits for them, and re-layouts, play_sample(): all_to_all(small, axis_name=mesh_name, split_axis=0, concat_axis=0)  11.2 us
    all_to_all x1, starting transfers between devices, play_sample(): all_to_all(small, axis_name=mesh_name, split_axis=0, concat_axis=0)  7.56 us
    dot_general x1, matrix products, body(): jnp.einsum('lk,qkc->qlc', inverse_table(), cross, preferred_element_type=...  7.23 us
  transfers between devices with their start and end apart: 1, of which 1 were waited for; matrix products, arithmetic and copies ran while one was open for 1% of the time, Pallas kernels for 0%

profile of v1, /device:TPU:0, one launch (start us, length us, event | category | flops | bytes accessed | tf_op | source)
XLA Modules:
  0.0 357.0 jit_solution(10420531642395725895)
XLA Ops:
  0.0 10.8 %copy.23 = bf16[896,4096]{0,1:T(8,128)(2,1)} copy(bf16[896,4096]{1,0:T(8,128)(2,1)} %param.3) | data formatting | bytes 14680064 | tf_op args[0]
  10.8 2.0 fusion.30
  12.8 2.3 fusion.29
  15.0 1.9 fusion.28
  16.9 1.9 fusion.27
  18.8 1.8 fusion.26
  20.6 1.8 fusion.25
  22.5 1.8 fusion.24
  24.3 1.9 fusion.23
  26.1 0.0 copy-done
  26.1 0.8 fusion.22
  27.0 0.8 fusion.21
  27.8 0.8 fusion.20
  28.6 0.8 fusion.19
  29.4 0.8 fusion.18
  30.2 0.8 fusion.17
  31.1 0.8 fusion.16
  31.9 0.8 fusion.15
  32.7 7.6 %all-to-all-start = ((bf16[16,896,1,256]{1,3,2,0:T(8,128)(2,1)}), bf16[16,896,1,256]{1,3,2,0:T(8,128)(2,1)}, u32[]{:S(2)}, u32[]{:S(2)}) async-start(bf16[16,896,1,256]{1,3,2,0:T(8,128)(2,1)} %fusion.15), calls=%async_computation | async-start | bytes 14680064 | tf_op jit(solution)/shard_map/all_to_all | solution.py:20
  40.3 0.0 copy-done.4
  40.3 0.1 reshape.120
  40.4 0.1 reshape.119
  40.4 0.0 copy-done.3
  40.5 0.6 cosine_convert_fusion
  41.1 1.1 fusion.45
  42.2 130.5 %all-to-all-done = bf16[16,896,1,256]{1,3,2,0:T(8,128)(2,1)} async-done(((bf16[16,896,1,256]{1,3,2,0:T(8,128)(2,1)}), bf16[16,896,1,256]{1,3,2,0:T(8,128)(2,1)}, u32[]{:S(2)}, u32[]{:S(2)}) %all-to-all-start) | async-done | bytes 7340064 | tf_op jit(solution)/shard_map/all_to_all | solution.py:20
  172.7 11.2 %copy.26 = bf16[16,896,1,256]{3,1,0,2:T(8,128)(2,1)} copy(bf16[16,896,1,256]{1,3,2,0:T(8,128)(2,1)} %all-to-all-done) | data formatting | bytes 14680064 | tf_op jit(solution)/shard_map/all_to_all | solution.py:20
  183.9 5.2 %convolution_bitcast_fusion = f32[28,256,256]{1,2,0:T(8,128)S(1)} fusion(bf16[28,512,256]{2,1,0:T(8,128)(2,1)} %bitcast.88, f32[512,128]{1,0:T(8,128)S(1)} %get-tuple-element.12, f32[512,128]{1,0:T(8,128)S(1)} %get-tuple-element.11), kind=kOutput, calls=%fused_computation.13 | convolution fusion | flops 1879441408 | bytes 15204352 | tf_op jit(solution)/shard_map/tk,wtc->wkc/dot_general | solution.py:46
  189.1 0.5 fusion.3
  189.6 0.1 rsqrt_multiply_fusion
  189.7 1.0 multiply_convert_fusion.1
  190.7 4.2 %copy.28 = bf16[28,256,256]{1,0,2:T(8,128)(2,1)} copy(bf16[28,256,256]{1,2,0:T(8,128)(2,1)S(1)} %multiply_convert_fusion.1) | data formatting | bytes 7340032 | tf_op jit(solution)/shard_map/convert_element_type | solution.py:50
  194.8 2.9 fusion.52
  197.7 2.8 gather_fusion
  200.5 3.4 copy.29
  203.9 2.7 convert_select_fusion
  206.6 122.9 %all-reduce.1 = bf16[32,28,256]{1,0,2:T(8,128)(2,1)S(1)} all-reduce(f32[32,28,256]{1,0,2:T(8,128)} %convert_select_fusion), channel_id=1, replica_groups=mesh['groups'=2,'chan'=16] {'chan'}, use_global_device_ids=true, to_apply=%region_1.2 | all-reduce | flops 229376 | bytes 1376256 | tf_op jit(solution)/shard_map/psum | solution.py:57
  329.5 4.5 %copy.30 = bf16[28,128,256]{2,0,1:T(8,128)(2,1)} copy(bf16[28,128,256]{1,2,0:T(8,128)(2,1)} %get-tuple-element.5) | data formatting | bytes 3670016 | tf_op jit(solution)/shard_map/slice | solution.py:59
  334.0 4.4 %copy.31 = bf16[28,128,256]{2,0,1:T(8,128)(2,1)} copy(bf16[28,128,256]{1,2,0:T(8,128)(2,1)} %get-tuple-element.6) | data formatting | bytes 3670016 | tf_op jit(solution)/shard_map/slice | solution.py:59
  338.4 2.4 fusion.12
  340.9 0.0 copy-done.2
  340.9 0.7 fusion.10
  341.6 0.7 fusion.6
  342.3 0.2 copy-done.1
  342.5 0.7 fusion.7
  343.2 0.4 pad_maximum_fusion
  343.5 7.2 %multiply_convert_fusion = bf16[32,256,256]{2,1,0:T(8,128)(2,1)} fusion(bf16[32,256,256]{2,0,1:T(8,128)(2,1)S(1)} %pad_maximum_fusion, bf16[256,128]{1,0:T(8,128)(2,1)S(1)} %get-tuple-element.8, bf16[256,128]{1,0:T(8,128)(2,1)S(1)} %get-tuple-element.7), kind=kOutput, calls=%fused_computation.1 | convolution fusion | flops 1078198272 | bytes 8519680 | tf_op jit(solution)/shard_map/lk,qkc->qlc/dot_general | solution.py:68
  350.8 6.2 %copy.35 = bf16[2,16,256,256]{3,2,1,0:T(8,128)(2,1)} copy(bf16[2,16,256,256]{2,3,1,0:T(8,128)(2,1)} %bitcast.105) | data formatting | bytes 8388608 | tf_op jit(solution)/shard_map/convert_element_type | solution.py:70
  (12 shorter events, 0.1 us)
Async XLA Ops:
  10.8 15.3 %copy-start = (bf16[896,4096]{0,1:T(8,128)(2,1)S(1)}, bf16[896,4096]{0,1:T(8,128)(2,1)}, u32[]{:S(2)}) copy-start(bf16[896,4096]{0,1:T(8,128)(2,1)} %copy.23) | copy-start | bytes 22020100
  32.7 7.6 %copy-start.4 = (s32[2,16]{1,0:T(2,128)S(1)}, s32[2,16]{1,0:T(2,128)}, u32[]{:S(2)}) copy-start(s32[2,16]{1,0:T(2,128)} %param.5) | copy-start | bytes 388
  32.7 7.8 %copy-start.3 = (s32[256]{0:T(256)S(1)}, s32[256]{0:T(256)}, u32[]{:S(2)}) copy-start(s32[256]{0:T(256)} %param.4) | copy-start | bytes 3076
  32.7 140.0 %all-to-all-start = ((bf16[16,896,1,256]{1,3,2,0:T(8,128)(2,1)}), bf16[16,896,1,256]{1,3,2,0:T(8,128)(2,1)}, u32[]{:S(2)}, u32[]{:S(2)}) async-start(bf16[16,896,1,256]{1,3,2,0:T(8,128)(2,1)} %fusion.15), calls=%async_computation | async-start | bytes 14680064 | tf_op jit(solution)/shard_map/all_to_all | solution.py:20
  338.4 2.4 copy-start.2
  340.9 1.6 copy-start.1
